TPU v7x, 32 devices: a whole 2x2x4 slice. The times are simulated.
32 devices in a mesh: cuts: 2 (over core), lx: 2 (over x), ly: 8 (over z, y).
Axes of the slice: x: 2, y: 2, z: 4, core: 2. Of those that a mesh axis runs over, the one named last changes fastest.
Arguments:
- disorder: int32 [16, 16, 128], P('lx', 'ly'), may hold values from 0 to 255
- slice_bounds: float32 [12, 2], P('cuts'), may hold values from -1.5 to 1.5
- start: float32 [12, 32, 16, 16, 128], P('cuts', None, 'lx', 'ly'), may hold values from -36 to 36
- ritz: float32 [12, 8, 16, 16, 128], P('cuts', None, 'lx', 'ly'), may hold values from -4 to 4
Outputs:
- block: float32 [12, 32, 16, 16, 128], P('cuts', None, 'lx', 'ly')
- correlations: float32 [12, 16, 32], P('cuts')
All inputs are finite; a program needn't handle non-finite values.
Results may differ from a plain program's by a relative error of at most 0.000096.
Values sent between devices are 32-bit elements; how exact they have to be, the bound alone decides.
A program may use at most 64 MiB of HBM per device.

v0:
```python
import jax
import jax.numpy as jnp
from jax import lax
from jax.sharding import PartitionSpec as P

LEVELS = 256


def passed_along(value, axis, steps):
    count = lax.axis_size(axis)
    first, last = (max(0, -steps), min(count, count - steps))
    return lax.ppermute(value, axis, [(source, source + steps) for source in range(first, last)])


def padded_2(block, sides, width):
    for axis, dim in sides:
        count = lax.axis_size(axis)
        forward = [(i, i + 1) for i in range(count - 1)]
        forward.append((count - 1, 0))
        backward = [(target, source) for source, target in forward]
        low = lax.ppermute(
            lax.slice_in_dim(block, block.shape[dim] - width, None, axis=dim), axis, forward
        )
        high = lax.ppermute(lax.slice_in_dim(block, 0, width, axis=dim), axis, backward)
        block = jnp.concatenate([low, block, high], axis=dim)
    return block


def apply_scaled(field, onsite, centre):
    inner = field[:, 1:-1, 1:-1]
    beside = field[:, 2:, 1:-1] + field[:, :-2, 1:-1]
    beside = beside + field[:, 1:-1, 2:] + field[:, 1:-1, :-2]
    beside = beside + jnp.roll(inner, 1, 3) + jnp.roll(inner, -1, 3)
    return ((onsite[None] - centre) * inner - beside) / 16.0


def on_device(disorder, slice_bounds, start, ritz):
    onsite = 16.5 * (disorder.astype(jnp.float32) / jnp.float32(LEVELS - 1) - 0.5)
    count = start.shape[0]
    width = start.shape[1]
    centre = jnp.repeat((slice_bounds[:, 0] + slice_bounds[:, 1]) / 2.0, width)[:, None, None, None]
    vectors = start.reshape((count * width,) + start.shape[2:])
    lower_edge = passed_along(ritz[-1:], "cuts", 1)
    upper_edge = passed_along(ritz[:1], "cuts", -1)
    lower = jnp.concatenate([lower_edge, ritz[:-1]], 0)
    upper = jnp.concatenate([ritz[1:], upper_edge], 0)

    def filter_step(field):
        padded = padded_2(field, (("lx", 1), ("ly", 2)), 1)
        return apply_scaled(padded, onsite, centre)

    previous = vectors
    current = filter_step(vectors)
    previous, current = (current, 2.0 * filter_step(current) - previous)
    shape = current.shape
    cells = shape[1] * shape[2] * shape[3]
    total = jnp.float32(cells * lax.axis_size("lx") * lax.axis_size("ly"))
    hp = lax.Precision.HIGHEST
    filtered = current.reshape(count, width, cells)
    window = jnp.concatenate([lower, upper], 1).reshape(count, 2 * ritz.shape[1], cells)
    summed = lax.psum(jnp.einsum("src,svc->srv", window, filtered, precision=hp), ("lx", "ly"))
    correlation = summed / total
    cleaned = filtered - jnp.einsum("srv,src->svc", correlation, window, precision=hp)
    gram = lax.psum(jnp.einsum("sac,sbc->sab", cleaned, cleaned, precision=hp), ("lx", "ly"))
    factor = jnp.linalg.cholesky(gram / total)
    result = jax.scipy.linalg.solve_triangular(factor, cleaned, lower=True)
    return (result.reshape((count, width) + shape[1:]), correlation)


def solution(mesh):
    in_specs = (
        P("lx", "ly", None),
        P("cuts", None),
        P("cuts", None, "lx", "ly", None),
        P("cuts", None, "lx", "ly", None),
    )
    out_specs = (P("cuts", None, "lx", "ly", None), P("cuts", None, None))
    return jax.shard_map(
        on_device, mesh=mesh, in_specs=in_specs, out_specs=out_specs, check_vma=False
    )
```

profile of v0, /device:TPU:0, one launch (start us, length us, event | category | flops | bytes accessed | tf_op | source)
XLA Modules:
  0.0 334.0 jit_solution(6009458818156026938)
XLA Ops:
  1.7 3.0 collective-permute-start
  10.5 3.4 %collective-permute-done.1 = f32[192,1,2,128]{3,2,1,0:T(2,128)S(1)} collective-permute-done((f32[192,1,2,128]{3,2,1,0:T(2,128)S(1)}, f32[192,1,2,128]{3,2,1,0:T(2,128)S(1)}, u32[]{:S(2)}, u32[]{:S(2)}) %collective-permute-start.1) | collective-permute-done | bytes 196640 | tf_op jit(solution)/shard_map/ppermute | solution.py:21
  18.1 4.9 %collective-permute-start.2 = (f32[192,10,1,128]{3,2,1,0:T(1,128)S(1)}, f32[192,10,1,128]{3,2,1,0:T(1,128)}, u32[]{:S(2)}, u32[]{:S(2)}) collective-permute-start(f32[192,10,1,128]{3,2,1,0:T(1,128)S(1)} %get-tuple-element.4), channel_id=1, source_target_pairs={{1,0},{2,1},{3,2},{4,3},{5,4},{6,5},{7,6},{0,7},{9,8},{10,9},{11,1... | collective-permute-start | bytes 2949128 | tf_op jit(solution)/shard_map/ppermute | solution.py:24
  23.8 2.1 fusion.23
  26.0 2.1 fusion.24
  28.2 34.1 %collective-permute-done.2 = f32[192,10,1,128]{3,2,1,0:T(1,128)} collective-permute-done((f32[192,10,1,128]{3,2,1,0:T(1,128)S(1)}, f32[192,10,1,128]{3,2,1,0:T(1,128)}, u32[]{:S(2)}, u32[]{:S(2)}) %collective-permute-start.2) | collective-permute-done | bytes 983072 | tf_op jit(solution)/shard_map/ppermute | solution.py:24
  62.3 9.1 %fusion.1 = f32[192,8,2,128]{3,2,1,0:T(2,128)S(1)} fusion(f32[192,8,2,128]{3,2,1,0:T(2,128)S(1)} %bitcast.24, f32[192,10,1,128]{3,2,1,0:T(1,128)} %collective-permute-done.3, f32[192,1,2,128]{3,2,1,0:T(2,128)S(1)} %copy-done.4, f32[192,1,2,128]{3,2,1,0:T(2,128)S(1)} %copy-done.6, f32[192,10,1,128]{3,2,1,0:T(1,128)} %collective-permute-done.2, ...), kind=kLoop, calls=%fused_computation.6 | loop fusion | flops 7471104 | bytes 8659712 | tf_op jit(solution)/shard_map/div | solution.py:34
  73.8 5.6 %collective-permute-done.4 = f32[192,1,2,128]{3,2,1,0:T(2,128)S(1)} collective-permute-done((f32[192,1,2,128]{3,2,1,0:T(2,128)S(1)}, f32[192,1,2,128]{3,2,1,0:T(2,128)S(1)}, u32[]{:S(2)}, u32[]{:S(2)}) %collective-permute-start.4) | collective-permute-done | bytes 196640 | tf_op jit(solution)/shard_map/ppermute | solution.py:24
  79.3 3.0 collective-permute-done.5
  83.3 2.8 fusion.18
  86.1 2.8 collective-permute-start.6
  88.9 2.1 maximum_maximum_fusion
  91.0 2.6 reshape.34
  93.6 2.1 fusion.20
  95.8 2.1 fusion.21
  98.0 33.2 %collective-permute-done.6 = f32[192,10,1,128]{3,2,1,0:T(1,128)} collective-permute-done((f32[192,10,1,128]{3,2,1,0:T(1,128)}, f32[192,10,1,128]{3,2,1,0:T(1,128)}, u32[]{:S(2)}, u32[]{:S(2)}) %collective-permute-start.6) | collective-permute-done | bytes 983072 | tf_op jit(solution)/shard_map/ppermute | solution.py:24
  131.1 10.1 %fusion.4 = f32[192,8,2,128]{3,2,1,0:T(2,128)} fusion(f32[192,8,2,128]{3,2,1,0:T(2,128)S(1)} %fusion.1, f32[192,10,1,128]{3,2,1,0:T(1,128)} %collective-permute-done.7, f32[192,1,2,128]{3,2,1,0:T(2,128)S(1)} %collective-permute-done.4, f32[192,1,2,128]{3,2,1,0:T(2,128)S(1)} %collective-permute-done.5, f32[192,10,1,128]{3,2,1,0:T(1,128)} %collective-permute-done.6, ...), kind=kLoop, calls=%fused_computation.9 | loop fusion | flops 7864320 | bytes 10232576 | tf_op jit(solution)/shard_map/sub | solution.py:54
  141.2 2.6 reshape.33
  145.2 75.1 %psum.14 = f32[6,16,32]{2,1,0:T(8,128)S(1)} all-reduce(f32[6,16,32]{2,1,0:T(8,128)S(1)} %fusion.28), channel_id=1, replica_groups=mesh['cuts'=2,'lx'=2,'ly'=8] {'lx','ly'}, use_global_device_ids=true, to_apply=%region_0.1 | all-reduce | flops 3072 | bytes 24576 | tf_op jit(solution)/shard_map/psum | solution.py:61
  220.4 2.6 convolution_subtract_fusion
  224.5 72.8 %psum.15 = f32[6,32,32]{1,2,0:T(8,128)S(1)} all-reduce(f32[6,32,32]{1,2,0:T(8,128)S(1)} %fusion.29), channel_id=1, replica_groups=mesh['cuts'=2,'lx'=2,'ly'=8] {'lx','ly'}, use_global_device_ids=true, to_apply=%region_1.2 | all-reduce | flops 6144 | bytes 49152 | tf_op jit(solution)/shard_map/psum | solution.py:64
  297.4 17.6 %custom-call.8 = f32[6,32,32]{2,1,0:T(8,128)S(1)} custom-call(f32[6,32,32]{2,1,0:T(8,128)S(1)} %fusion.17), custom_call_target="Cholesky" | custom-call | tf_op jit(solution)/shard_map/jit(cholesky)/cholesky | solution.py:65
  315.2 14.8 %custom-call.9 = f32[6,1,32,32]{2,3,1,0:T(8,128)S(1)} custom-call(f32[6,1,32,32]{3,2,1,0:T(8,128)S(1)} %select_bitcast_fusion), custom_call_target="InvertDiagBlocksLowerTriangular" | custom-call | tf_op jit(solution)/shard_map/jit(_solve_triangular)/vmap()/triangular_solve | solution.py:66
  331.5 2.5 reshape.35
  (57 shorter events, 20.0 us)
Async XLA Ops:
  1.7 8.8 %collective-permute-start = (f32[192,1,2,128]{3,2,1,0:T(2,128)S(1)}, f32[192,1,2,128]{3,2,1,0:T(2,128)S(1)}, u32[]{:S(2)}, u32[]{:S(2)}) collective-permute-start(f32[192,1,2,128]{3,2,1,0:T(2,128)S(1)} %get-tuple-element.17), channel_id=1, source_target_pairs={{8,0},{0,8},{9,1},{1,9},{10,2},{2,10},{11,3},{3,11},{12,4},{4,12},... | collective-permute-start | bytes 589832 | tf_op jit(solution)/shard_map/ppermute | solution.py:24
  4.7 9.1 %collective-permute-start.1 = (f32[192,1,2,128]{3,2,1,0:T(2,128)S(1)}, f32[192,1,2,128]{3,2,1,0:T(2,128)S(1)}, u32[]{:S(2)}, u32[]{:S(2)}) collective-permute-start(f32[192,1,2,128]{3,2,1,0:T(2,128)S(1)} %get-tuple-element.16), channel_id=1, source_target_pairs={{0,8},{8,0},{1,9},{9,1},{2,10},{10,2},{3,11},{11,3},{4,12},{12,4},... | collective-permute-start | bytes 589832 | tf_op jit(solution)/shard_map/ppermute | solution.py:21
  6.3 82.5 %collective-permute-start.8 = (f32[1,8,8,2,128]{4,3,2,1,0:T(2,128)}, f32[1,8,8,2,128]{4,3,2,1,0:T(2,128)}, u32[]{:S(2)}, u32[]{:S(2)}) collective-permute-start(f32[1,8,8,2,128]{4,3,2,1,0:T(2,128)} %get-tuple-element.18), channel_id=1, source_target_pairs={{0,16},{1,17},{2,18},{3,19},{4,20},{5,21},{6,22},{7,23},{8,24},{9,... | collective-permute-start | bytes 196616 | tf_op jit(solution)/shard_map/ppermute | solution.py:12
  8.4 80.5 %collective-permute-start.9 = (f32[1,8,8,2,128]{4,3,2,1,0:T(2,128)}, f32[1,8,8,2,128]{4,3,2,1,0:T(2,128)}, u32[]{:S(2)}, u32[]{:S(2)}) collective-permute-start(f32[1,8,8,2,128]{4,3,2,1,0:T(2,128)} %get-tuple-element.19), channel_id=1, source_target_pairs={{16,0},{17,1},{18,2},{19,3},{20,4},{21,5},{22,6},{23,7},{24,8},{25... | collective-permute-start | bytes 196616 | tf_op jit(solution)/shard_map/ppermute | solution.py:12
  10.5 3.4 %copy-start.3 = (f32[192,1,2,128]{3,2,1,0:T(2,128)}, f32[192,1,2,128]{3,2,1,0:T(2,128)S(1)}, u32[]{:S(2)}) copy-start(f32[192,1,2,128]{3,2,1,0:T(2,128)S(1)} %collective-permute-done) | copy-start | bytes 589828
  13.8 0.7 copy-start.5
  16.5 6.4 %copy-start.10 = (f32[6,2]{0,1:T(2,128)S(1)}, f32[6,2]{0,1:T(2,128)}, u32[]{:S(2)}) copy-start(f32[6,2]{0,1:T(2,128)} %param.5) | copy-start | bytes 148
  16.6 7.3 %copy-start = (f32[6,32,8,2,128]{4,3,2,1,0:T(2,128)S(1)}, f32[6,32,8,2,128]{4,3,2,1,0:T(2,128)}, u32[]{:S(2)}) copy-start(f32[6,32,8,2,128]{4,3,2,1,0:T(2,128)} %param.6) | copy-start | bytes 4718596
  18.1 44.1 %collective-permute-start.2 = (f32[192,10,1,128]{3,2,1,0:T(1,128)S(1)}, f32[192,10,1,128]{3,2,1,0:T(1,128)}, u32[]{:S(2)}, u32[]{:S(2)}) collective-permute-start(f32[192,10,1,128]{3,2,1,0:T(1,128)S(1)} %get-tuple-element.4), channel_id=1, source_target_pairs={{1,0},{2,1},{3,2},{4,3},{5,4},{6,5},{7,6},{0,7},{9,8},{10,9},{11,1... | collective-permute-start | bytes 2949128 | tf_op jit(solution)/shard_map/ppermute | solution.py:24
  23.0 39.3 %collective-permute-start.3 = (f32[192,10,1,128]{3,2,1,0:T(1,128)S(1)}, f32[192,10,1,128]{3,2,1,0:T(1,128)}, u32[]{:S(2)}, u32[]{:S(2)}) collective-permute-start(f32[192,10,1,128]{3,2,1,0:T(1,128)S(1)} %get-tuple-element.5), channel_id=1, source_target_pairs={{0,1},{1,2},{2,3},{3,4},{4,5},{5,6},{6,7},{7,0},{8,9},{9,10},{10,1... | collective-permute-start | bytes 2949128 | tf_op jit(solution)/shard_map/ppermute | solution.py:21
  23.1 39.1 %copy-start.8 = (f32[192]{0:T(256)}, f32[192]{0:T(256)S(1)}, u32[]{:S(2)}) copy-start(f32[192]{0:T(256)S(1)} %sub.40) | copy-start | bytes 2308
  26.0 36.3 %copy-start.4 = (f32[192,1,2,128]{3,2,1,0:T(2,128)S(1)}, f32[192,1,2,128]{3,2,1,0:T(2,128)}, u32[]{:S(2)}) copy-start(f32[192,1,2,128]{3,2,1,0:T(2,128)} %copy-done.3) | copy-start | bytes 589828
  26.0 36.3 %copy-start.6 = (f32[192,1,2,128]{3,2,1,0:T(2,128)S(1)}, f32[192,1,2,128]{3,2,1,0:T(2,128)}, u32[]{:S(2)}) copy-start(f32[192,1,2,128]{3,2,1,0:T(2,128)} %copy-done.5) | copy-start | bytes 589828
  62.3 11.3 %copy-start.2 = (f32[6,8,8,2,128]{4,3,2,1,0:T(2,128)S(1)}, f32[6,8,8,2,128]{4,3,2,1,0:T(2,128)}, u32[]{:S(2)}) copy-start(f32[6,8,8,2,128]{4,3,2,1,0:T(2,128)} %param.7) | copy-start | bytes 1179652
  71.5 7.8 %collective-permute-start.4 = (f32[192,1,2,128]{3,2,1,0:T(2,128)S(1)}, f32[192,1,2,128]{3,2,1,0:T(2,128)S(1)}, u32[]{:S(2)}, u32[]{:S(2)}) collective-permute-start(f32[192,1,2,128]{3,2,1,0:T(2,128)S(1)} %get-tuple-element.11), channel_id=1, source_target_pairs={{8,0},{0,8},{9,1},{1,9},{10,2},{2,10},{11,3},{3,11},{12,4},{4,12},... | collective-permute-start | bytes 589832 | tf_op jit(solution)/shard_map/ppermute | solution.py:24
  73.0 9.4 %collective-permute-start.5 = (f32[192,1,2,128]{3,2,1,0:T(2,128)S(1)}, f32[192,1,2,128]{3,2,1,0:T(2,128)S(1)}, u32[]{:S(2)}, u32[]{:S(2)}) collective-permute-start(f32[192,1,2,128]{3,2,1,0:T(2,128)S(1)} %get-tuple-element.10), channel_id=1, source_target_pairs={{0,8},{8,0},{1,9},{9,1},{2,10},{10,2},{3,11},{11,3},{4,12},{12,4},... | collective-permute-start | bytes 589832 | tf_op jit(solution)/shard_map/ppermute | solution.py:21
  86.1 45.1 %collective-permute-start.6 = (f32[192,10,1,128]{3,2,1,0:T(1,128)}, f32[192,10,1,128]{3,2,1,0:T(1,128)}, u32[]{:S(2)}, u32[]{:S(2)}) collective-permute-start(f32[192,10,1,128]{3,2,1,0:T(1,128)} %get-tuple-element.2), channel_id=1, source_target_pairs={{1,0},{2,1},{3,2},{4,3},{5,4},{6,5},{7,6},{0,7},{9,8},{10,9},{11,1... | collective-permute-start | bytes 2949128 | tf_op jit(solution)/shard_map/ppermute | solution.py:24
  88.9 42.3 %collective-permute-start.7 = (f32[192,10,1,128]{3,2,1,0:T(1,128)}, f32[192,10,1,128]{3,2,1,0:T(1,128)}, u32[]{:S(2)}, u32[]{:S(2)}) collective-permute-start(f32[192,10,1,128]{3,2,1,0:T(1,128)} %get-tuple-element.3), channel_id=1, source_target_pairs={{0,1},{1,2},{2,3},{3,4},{4,5},{5,6},{6,7},{7,0},{8,9},{9,10},{10,1... | collective-permute-start | bytes 2949128 | tf_op jit(solution)/shard_map/ppermute | solution.py:21
  95.8 35.3 %copy-start.9 = (f32[192]{0:T(256)S(1)}, f32[192]{0:T(256)}, u32[]{:S(2)}) copy-start(f32[192]{0:T(256)} %copy-done.8) | copy-start | bytes 2308
  141.2 2.6 copy-start.1
  220.3 2.6 copy-start.7
where the time goes:
time: 335 us; the launch traced here: 334 us
  blocking collectives  148 us (44%)
  waiting for transfers between devices  80 us (24%)
  other arithmetic  57.5 us (17%)
  local copies, waits for them, and re-layouts  24.5 us (7%)
  starting transfers between devices  16.2 us (5%)
  matrix products  6.98 us (2%)
    psum x1, blocking collectives, on_device(): lax.psum(jnp.einsum('src,svc->srv', window, filtered, precision=hp), ('lx...  75.1 us
    ppermute x4, waiting for transfers between devices, padded_2(): lax.ppermute(lax.slice_in_dim(block, 0, width, axis=dim), axis, backward)  73.6 us
    psum x1, blocking collectives, on_device(): lax.psum(jnp.einsum('sac,sbc->sab', cleaned, cleaned, precision=hp), ('lx...  72.8 us
    another operation x4, other arithmetic, on_device(): factor = jnp.linalg.cholesky(gram / total)  17.7 us
    another operation x3, other arithmetic, on_device(): result = jax.scipy.linalg.solve_triangular(factor, cleaned, lower=True)  14.9 us
    ppermute x4, starting transfers between devices, padded_2(): lax.ppermute(lax.slice_in_dim(block, 0, width, axis=dim), axis, backward)  12.2 us
    sub x1, other arithmetic, on_device(): previous, current = (current, 2.0 * filter_step(current) - previous)  10.1 us
    div x1, other arithmetic, apply_scaled(): return ((onsite[None] - centre) * inner - beside) / 16.0  9.07 us
  transfers between devices with their start and end apart: 10, of which 6 were waited for; matrix products, arithmetic and copies ran while one was open for 10% of the time, Pallas kernels for 0%

commit v1 on v0

v1 whole, which is shorter than its diff:
```python
import functools

import jax
import jax.numpy as jnp
from jax import lax
from jax.experimental import pallas as pl
from jax.experimental.pallas import tpu as pltpu
from jax.sharding import PartitionSpec as P

LEVELS = 256
MESH = pl.DeviceIdType.MESH
HP = lax.Precision.HIGHEST
H = 2


def kernel(dims, dis, bnd, start, ritz, out, cor, E, T, O, U, FA, FT, RA, ACC, LM, PK, RX, RZ, SM, AL,
           hs, hr, fs, fr, rs, rr, xs, xr, zs, zr, gs, gr):
    nc, nx, ny, count, NV, NR, X, Y, NZ = dims
    S = count // 2
    R = 2 * Y
    J = X * Y
    K = ny // 2
    ng = nx * 2
    tg = RX.shape[1]
    tiles = ng * tg
    total = float(J * NZ * nx * ny)
    cut, mx, my = lax.axis_index("cuts"), lax.axis_index("lx"), lax.axis_index("ly")
    p = lax.rem(my, 2)
    q = 1 - p
    kz = my // 2
    g = mx * 2 + p
    partner = kz * 2 + q
    zup = lax.rem(kz + 1, K) * 2 + p
    zdown = lax.rem(kz + K - 1, K) * 2 + p
    xup = lax.rem(mx + 1, nx)
    xdown = lax.rem(mx + nx - 1, nx)

    barrier = pltpu.get_barrier_semaphore()

    def greet(dev):
        pl.semaphore_signal(barrier, inc=1, device_id=dev, device_id_type=MESH)

    def in_plane(o):
        t = lax.rem(g + o, ng)
        return t, (cut, t // 2, kz * 2 + lax.rem(t, 2))

    def in_line(o):
        t = lax.rem(kz + o, K)
        return t, (cut, mx, t * 2 + p)

    for o in range(1, ng):
        greet(in_plane(o)[1])
    for o in range(1, K):
        greet(in_line(o)[1])
    cup = (lax.rem(cut + 1, nc), mx, my)
    cdown = (lax.rem(cut + nc - 1, nc), mx, my)
    greet(cup)
    greet(cdown)

    lo = H + Y * p
    for x in range(X):
        for r in range(Y):
            row = dis[pl.ds(x * Y + r, 1), :].astype(jnp.float32)
            row = 16.5 * (row / jnp.float32(LEVELS - 1) - 0.5)
            O[H + x, lo + r] = jnp.broadcast_to(row, (8, NZ))
    for c in range(S):
        for x in range(X):
            for r in range(Y):
                pick = pl.ds(x * Y + r, NV, stride=J)
                T[c, x, r] = start[q * S + c, pick, :]
                E[c, H + x, lo + r] = start[p * S + c, pick, :]
    for s in range(count):
        for x in range(X):
            for r in range(Y):
                RA[s + 1, x, r] = ritz[s, pl.ds(x * Y + r, NR, stride=J), :]
    pl.semaphore_wait(barrier, ng + K)

    pending = []

    def send(src, dst, ss, rs_, dev):
        copy = pltpu.make_async_remote_copy(
            src_ref=src, dst_ref=dst, send_sem=ss, recv_sem=rs_, device_id=dev, device_id_type=MESH)
        copy.start()
        pending.append(copy)

    def arrived(dst, rs_):
        pltpu.make_async_remote_copy(
            src_ref=dst, dst_ref=dst, send_sem=rs_, recv_sem=rs_,
            device_id=(cut, mx, partner), device_id_type=MESH).wait_recv()

    fields = [(S, O)] + [(c, E.at[c]) for c in range(S)]
    xi = pl.ds(H, X)
    xy = (cut, mx, partner)

    def row_block(at):
        return pl.ds(at, Y)

    def send_rows(c, buf, half):
        up = half
        target = jnp.where(up == 1, zup, zdown)
        dst_row = jnp.where(up == 1, 0, H + R)
        side = 1 - up
        send(buf.at[xi, row_block(H + Y * half)], buf.at[xi, row_block(dst_row)],
             hs.at[c, 1 + side], hr.at[c, 1 + side], (cut, mx, target))

    for c, buf in fields:
        src = buf.at[xi, row_block(lo)] if c == S else T.at[c]
        send(src, buf.at[xi, row_block(lo)], hs.at[c, 0], hr.at[c, 0], xy)
    for c, buf in fields:
        send_rows(c, buf, p)
    send(RA.at[count], RA.at[0], rs.at[0], rr.at[0], cup)
    send(RA.at[1], RA.at[count + 1], rs.at[1], rr.at[1], cdown)

    own = pl.ds(H, R)
    for c, buf in fields:
        arrived(buf.at[xi, row_block(H + Y * q)], hr.at[c, 0])
        send_rows(c, buf, q)
        send(buf.at[pl.ds(X, H), own], buf.at[pl.ds(0, H), own], hs.at[c, 3], hr.at[c, 3], (cut, xup, my))
        send(buf.at[pl.ds(H, H), own], buf.at[pl.ds(H + X, H), own], hs.at[c, 4], hr.at[c, 4], (cut, xdown, my))

    def point(src, c, x, r, centre):
        v = src(x, r)
        beside = src(x + 1, r) + src(x - 1, r)
        beside = beside + src(x, r + 1) + src(x, r - 1)
        beside = beside + pltpu.roll(v, 1, 1) + pltpu.roll(v, NZ - 1, 1)
        level = O[x, r] - centre
        level = jnp.concatenate([level] * (NV // 8), 0)
        return (level * v - beside) * 0.0625

    for c, buf in fields:
        for side, row in ((0, 0), (1, H + R)):
            arrived(buf.at[xi, row_block(row)], hr.at[c, 1 + side])
        for side, row in ((0, 1), (1, H + R)):
            send(buf.at[H + X - 1, row], buf.at[1, row], hs.at[c, 5 + 2 * side], hr.at[c, 5 + 2 * side], (cut, xup, my))
            send(buf.at[H, row], buf.at[H + X, row], hs.at[c, 6 + 2 * side], hr.at[c, 6 + 2 * side], (cut, xdown, my))
        arrived(buf.at[pl.ds(0, H), own], hr.at[c, 3])
        arrived(buf.at[pl.ds(H + X, H), own], hr.at[c, 4])
        for side, row in ((0, 1), (1, H + R)):
            arrived(buf.at[1, row], hr.at[c, 5 + 2 * side])
            arrived(buf.at[H + X, row], hr.at[c, 6 + 2 * side])
        if c == S:
            continue
        s = p * S + c
        centre = (bnd[s, 0] + bnd[s, 1]) / 2.0

        def from_e(x, r, c=c):
            return E[c, x, r]

        def from_u(x, r):
            return U[x, r]

        for x in (1, H + X):
            for r in range(H, H + R):
                U[x, r] = point(from_e, c, x, r, centre)

        def first(i, carry, c=c, centre=centre):
            for r in range(1, H + R + 1):
                U[H + i, r] = point(from_e, c, H + i, r, centre)
            return carry

        lax.fori_loop(0, X, first, 0)

        def second(i, carry, c=c, s=s, centre=centre):
            for r in range(Y):
                a = H + Y * p + r
                FA[s, i, r] = 2.0 * point(from_u, c, H + i, a, centre) - E[c, H + i, a]
                b = H + Y * q + r
                FT[c, i, r] = 2.0 * point(from_u, c, H + i, b, centre) - E[c, H + i, b]
            return carry

        lax.fori_loop(0, X, second, 0)
        send(FT.at[c], FA.at[s], fs.at[c], fr.at[c], xy)

    arrived(RA.at[0], rr.at[0])
    arrived(RA.at[count + 1], rr.at[1])

    @pl.when(cut == 0)
    def _():
        RA[0] = jnp.zeros((X, Y, NR, NZ), jnp.float32)

    @pl.when(cut == nc - 1)
    def _():
        RA[count + 1] = jnp.zeros((X, Y, NR, NZ), jnp.float32)

    for c in range(S):
        arrived(FA.at[q * S + c], fr.at[c])

    contract = (((1,), (1,)), ((), ()))
    ACC[...] = jnp.zeros(ACC.shape, jnp.float32)

    def grams(i, carry):
        z = [jnp.concatenate([FA[s, i, r] for s in range(count)] + [RA[t, i, r] for t in range(count + 2)], 0)
             for r in range(Y)]
        z = jnp.concatenate(z, 1)
        ACC[...] += lax.dot_general(z, z, contract, precision=HP, preferred_element_type=jnp.float32)
        return carry

    lax.fori_loop(0, X, grams, 0)

    NL = ACC.shape[1]
    base = count * NV
    lane = lax.broadcasted_iota(jnp.int32, (8, NL), 1)

    def masked(row, first, width):
        keep = jnp.logical_and(lane >= first, lane < first + width)
        return jnp.where(keep, ACC[pl.ds(row, 8), :], 0.0)

    packed = []
    for b in range(NV // 8):
        acc = jnp.zeros((8, NL), jnp.float32)
        for s in range(count):
            acc = acc + masked(s * NV + b * 8, s * NV, NV)
        if b == 0:
            for t in range(count + 2):
                acc = acc + masked(base + t * NR, base + t * NR, NR)
        if b == 1:
            for s in range(count):
                acc = acc + masked(base + s * NR, base + (s + 2) * NR, NR)
        if b == 2:
            for s in range(count):
                acc = acc + masked(base + (s + 2) * NR, base + s * NR, NR)
        packed.append(acc)
    for b in range(2):
        acc = jnp.zeros((8, NL), jnp.float32)
        for s in range(count):
            acc = acc + masked(base + (s + 2 * b) * NR, s * NV, NV)
        packed.append(acc)
    halves = NL // 128
    used = len(packed) * halves
    for i in range(tiles):
        if i < used:
            h = i % halves
            PK[i] = packed[i // halves][:, h * 128:(h + 1) * 128]
        else:
            PK[i] = jnp.zeros((8, 128), jnp.float32)

    RX[g] = PK[pl.ds(g * tg, tg)]
    for o in range(1, ng):
        t, dev = in_plane(o)
        send(PK.at[pl.ds(t * tg, tg)], RX.at[g], xs.at[o], xr.at[g], dev)
    for o in range(1, ng):
        t, _ = in_plane(o)
        arrived(RX.at[t], xr.at[t])
    mine = RX[0]
    for t in range(1, ng):
        mine = mine + RX[t]
    RZ[kz] = mine
    SM[...] = mine
    for o in range(1, K):
        t, dev = in_line(o)
        send(SM, RZ.at[kz], zs.at[o], zr.at[kz], dev)
    for o in range(1, K):
        t, _ = in_line(o)
        arrived(RZ.at[t], zr.at[t])
    mine = RZ[0]
    for t in range(1, K):
        mine = mine + RZ[t]
    AL[g] = mine
    for o in range(1, ng):
        t, dev = in_plane(o)
        send(AL.at[g], AL.at[g], gs.at[o], gr.at[g], dev)
    for o in range(1, ng):
        t, _ = in_plane(o)
        arrived(AL.at[t], gr.at[t])

    def tile(row, first):
        i = row * halves + first // 128
        value = AL[i // tg, i % tg] * (1.0 / total)
        shift = first % 128
        return pltpu.roll(value, 128 - shift, 1) if shift else value

    l8 = lax.broadcasted_iota(jnp.int32, (8, 128), 1)
    l32 = lax.broadcasted_iota(jnp.int32, (NV, 128), 1)
    r32 = lax.broadcasted_iota(jnp.int32, (NV, 128), 0)
    eye = jnp.where(l32 == r32 + NV, 1.0, 0.0)
    e16r = lax.broadcasted_iota(jnp.int32, (2 * NR, 128), 0)
    e16l = lax.broadcasted_iota(jnp.int32, (2 * NR, 128), 1)
    corrs, mats = [], []
    for s in range(count):
        corr = jnp.concatenate([tile(NV // 8 + b, s * NV) for b in range(2)], 0)[:, :NV]
        corrs.append(corr)
        cor[s] = corr
        a00 = tile(0, base + s * NR)
        a11 = pltpu.roll(tile(0, base + (s + 2) * NR), NR, 1)
        a01 = pltpu.roll(tile(1, base + (s + 2) * NR), NR, 1)
        a10 = tile(2, base + s * NR)
        b = jnp.concatenate([jnp.where(l8 < NR, a00, a01), jnp.where(l8 < NR, a10, a11)], 0)
        b = jnp.where(e16r == e16l, 2.0, 0.0) - b
        b = b[:, :2 * NR]
        bc = lax.dot_general(b, corr, (((1,), (0,)), ((), ())), precision=HP, preferred_element_type=jnp.float32)
        sub = lax.dot_general(corr, bc, (((0,), (0,)), ((), ())), precision=HP, preferred_element_type=jnp.float32)
        ff = jnp.concatenate([tile(b_, s * NV) for b_ in range(NV // 8)], 0)
        sub = jnp.concatenate([sub, jnp.zeros((NV, 128 - NV), jnp.float32)], 1)
        mats.append(jnp.where(l32 < NV, ff - sub, eye)[None])
    M = jnp.concatenate(mats, 0)
    rows = lax.broadcasted_iota(jnp.int32, (1, NV, 1), 1)
    for k in range(NV):
        pivot = M[:, k:k + 1, :]
        inv = 1.0 / pivot[:, :, k:k + 1]
        f = jnp.where(rows > k, M[:, :, k:k + 1] * inv, 0.0)
        M = M - f * pivot
    diag = jnp.sum(jnp.where(l32[None] == r32[None], M, 0.0), axis=2, keepdims=True)
    M = M * (1.0 / jnp.sqrt(diag))
    ident = jnp.where(l32 == r32, 1.0, 0.0)[:, :NV]
    for s in range(count):
        linv = pltpu.roll(M[s], 128 - NV, 1)[:, :NV]
        full = jnp.concatenate([ident, -corrs[s]], 0)
        LM[s] = lax.dot_general(linv, full, contract, precision=HP, preferred_element_type=jnp.float32)

    def finish(s, carry):
        left = LM[s]
        for x in range(X):
            z = [jnp.concatenate([FA[s, x, r], RA[s, x, r], RA[s + 2, x, r]], 0) for r in range(Y)]
            z = jnp.concatenate(z, 1)
            o = lax.dot_general(left, z, (((1,), (0,)), ((), ())), precision=HP, preferred_element_type=jnp.float32)
            for r in range(Y):
                out[s, pl.ds(x * Y + r, NV, stride=J), :] = o[:, r * NZ:(r + 1) * NZ]
        return carry

    lax.fori_loop(0, count, finish, 0)
    for copy in pending:
        copy.wait_send()


def on_device(disorder, slice_bounds, start, ritz):
    nc, nx, ny = (lax.axis_size(a) for a in ("cuts", "lx", "ly"))
    count, NV, X, Y, NZ = start.shape
    NR = ritz.shape[1]
    J = X * Y
    S, R, K, ng = count // 2, 2 * Y, ny // 2, nx * 2
    NL = count * NV + (count + 2) * NR
    tg = -(-((NV + 2 * NR) // 8 * (NL // 128)) // ng)
    f32 = jnp.float32
    V = pltpu.VMEM
    D = pltpu.SemaphoreType.DMA
    dims = (nc, nx, ny, count, NV, NR, X, Y, NZ)
    vm = pl.BlockSpec(memory_space=pltpu.VMEM)
    block, corr = pl.pallas_call(
        functools.partial(kernel, dims),
        out_shape=(jax.ShapeDtypeStruct((count, NV * J, NZ), f32),
                   jax.ShapeDtypeStruct((count, 2 * NR, NV), f32)),
        in_specs=[vm, pl.BlockSpec(memory_space=pltpu.SMEM), vm, vm],
        out_specs=(vm, vm),
        scratch_shapes=[
            V((S, X + 2 * H, R + 2 * H, NV, NZ), f32),
            V((S, X, Y, NV, NZ), f32),
            V((X + 2 * H, R + 2 * H, 8, NZ), f32),
            V((X + 2 * H, R + 2 * H, NV, NZ), f32),
            V((count, X, Y, NV, NZ), f32),
            V((S, X, Y, NV, NZ), f32),
            V((count + 2, X, Y, NR, NZ), f32),
            V((NL, NL), f32),
            V((count, NV, NV + 2 * NR), f32),
            V((ng * tg, 8, 128), f32),
            V((ng, tg, 8, 128), f32),
            V((K, tg, 8, 128), f32),
            V((tg, 8, 128), f32),
            V((ng, tg, 8, 128), f32),
            D((S + 1, 9)), D((S + 1, 9)), D((S,)), D((S,)), D((2,)), D((2,)),
            D((ng,)), D((ng,)), D((K,)), D((K,)), D((ng,)), D((ng,)),
        ],
        compiler_params=pltpu.CompilerParams(collective_id=0, has_side_effects=True, vmem_limit_bytes=48 << 20),
    )(disorder.reshape(J, NZ), slice_bounds, start.reshape(count, NV * J, NZ), ritz.reshape(count, NR * J, NZ))
    return (block.reshape(start.shape), corr)


def solution(mesh):
    in_specs = (
        P("lx", "ly", None),
        P("cuts", None),
        P("cuts", None, "lx", "ly", None),
        P("cuts", None, "lx", "ly", None),
    )
    out_specs = (P("cuts", None, "lx", "ly", None), P("cuts", None, None))
    return jax.shard_map(
        on_device, mesh=mesh, in_specs=in_specs, out_specs=out_specs, check_vma=False
    )
```

time: 335 us -> 84.3 us (0.25)
  blocking collectives: 148 us -> 0 us
  waiting for transfers between devices: 80 us -> 0 us
  Pallas kernels: 0 us -> 77.7 us
  other arithmetic: 57.5 us -> 0 us
  local copies, waits for them, and re-layouts: 24.5 us -> 5.63 us
  starting transfers between devices: 16.2 us -> 0 us
  matrix products: 6.98 us -> 0 us
    psum x2 -> x0, blocking collectives: 148 us -> none  [the longest x1 75.1 us: on_device(): lax.psum(jnp.einsum('src,svc->srv', window, filtered, precision=hp), ('lx...]
    ppermute x10 -> x0, waiting for transfers between devices: 80 us -> none  [the longest x4 73.6 us: padded_2(): lax.ppermute(lax.slice_in_dim(block, 0, width, axis=dim), axis, backward)]
    pallas_call x0 -> x1, Pallas kernels: none -> 77.7 us  [on_device(): pl.pallas_call(functools.partial(kernel, dims), out_shape=(jax.ShapeDtype...]
    another operation x7 -> x0, other arithmetic: 32.6 us -> none  [the longest x4 17.7 us: on_device(): factor = jnp.linalg.cholesky(gram / total)]
    ppermute x10 -> x0, starting transfers between devices: 16.2 us -> none  [the longest x4 12.2 us: padded_2(): lax.ppermute(lax.slice_in_dim(block, 0, width, axis=dim), axis, backward)]
    slice x10 -> x0, local copies, waits for them, and re-layouts: 15.8 us -> none  [the longest x4 8.56 us: apply_scaled(): beside = beside + jnp.roll(inner, 1, 3) + jnp.roll(inner, -1, 3)]
    sub x1 -> x0, other arithmetic: 10.1 us -> none  [on_device(): previous, current = (current, 2.0 * filter_step(current) - previous)]
    div x5 -> x0, other arithmetic: 9.11 us -> none  [the longest x1 9.07 us: apply_scaled(): return ((onsite[None] - centre) * inner - beside) / 16.0]
  transfers between devices with their start and end apart: 10 -> 0, of which waited for: 6 -> 0; matrix products, arithmetic and copies ran while one was open for 10% -> 0% of each run, Pallas kernels for 0% -> 0%
where the time goes in v1:
time: 84.3 us; the launch traced here: 84 us
  Pallas kernels  77.7 us (92%)
  local copies, waits for them, and re-layouts  5.63 us (7%)
    pallas_call x1, Pallas kernels, on_device(): pl.pallas_call(functools.partial(kernel, dims), out_shape=(jax.ShapeDtype...  77.7 us
    unnamed x9, local copies, waits for them, and re-layouts  5.63 us

profile of v1, /device:TPU:0, one launch (start us, length us, event | category | flops | bytes accessed | tf_op | source)
XLA Modules:
  0.0 84.0 jit_solution(14051646664322597175)
XLA Ops:
  0.6 0.8 copy.6.bnd
  1.4 0.0 copy-start
  1.4 1.4 %copy-done = f32[6,32,8,2,128]{4,3,2,1,0:T(2,128)S(1)} copy-done((f32[6,32,8,2,128]{4,3,2,1,0:T(2,128)S(1)}, f32[6,32,8,2,128]{4,3,2,1,0:T(2,128)}, u32[]{:S(2)}) %copy-start) | copy-done | bytes 1572888
  2.8 0.0 copy-start.1
  2.8 1.0 %copy-done.1 = f32[6,8,8,2,128]{4,3,2,1,0:T(2,128)S(1)} copy-done((f32[6,8,8,2,128]{4,3,2,1,0:T(2,128)S(1)}, f32[6,8,8,2,128]{4,3,2,1,0:T(2,128)}, u32[]{:S(2)}) %copy-start.1) | copy-done | bytes 393240
  3.8 0.0 copy-start.2
  3.8 0.7 copy-done.2
  4.5 77.7 %shard_map.59 = (f32[6,512,128]{2,1,0:T(8,128)S(1)}, f32[6,16,32]{2,1,0:T(8,128)S(1)}) custom-call(s32[16,128]{1,0:T(8,128)S(1)} %bitcast.7, f32[6,2]{1,0:T(8,128)S(1)} %copy.6.bnd, f32[6,512,128]{2,1,0:T(8,128)S(1)} %bitcast.5, f32[6,128,128]{2,1,0:T(8,128)S(1)} %bitcast.6), custom_call_target="tpu_custom_call" | custom-call | tf_op jit(solution)/shard_map/pallas_call | solution.py:338
  82.3 1.1 %copy.9 = f32[6,32,8,2,128]{4,3,2,1,0:T(2,128)} copy(f32[6,32,8,2,128]{4,3,2,1,0:T(2,128)S(1)} %bitcast.4) | data formatting | bytes 3145728
  83.4 0.6 copy.10
Async XLA Ops:
  1.4 1.4 %copy-start = (f32[6,32,8,2,128]{4,3,2,1,0:T(2,128)S(1)}, f32[6,32,8,2,128]{4,3,2,1,0:T(2,128)}, u32[]{:S(2)}) copy-start(f32[6,32,8,2,128]{4,3,2,1,0:T(2,128)} %param.6) | copy-start | bytes 4718596
  2.8 1.0 %copy-start.1 = (f32[6,8,8,2,128]{4,3,2,1,0:T(2,128)S(1)}, f32[6,8,8,2,128]{4,3,2,1,0:T(2,128)}, u32[]{:S(2)}) copy-start(f32[6,8,8,2,128]{4,3,2,1,0:T(2,128)} %param.7) | copy-start | bytes 1179652
  3.8 0.7 copy-start.2

commit v2 on v1

--- a/solution.py
+++ b/solution.py
@@ -13,10 +13,13 @@
 H = 2
 
 
-def kernel(dims, dis, bnd, start, ritz, out, cor, E, T, O, U, FA, FT, RA, ACC, LM, PK, RX, RZ, SM, AL,
+def kernel(dims, dis_h, bnd, start_h, ritz_h, out, cor, dis, start, ritz, ls, E, T, O, U, FA, FT, RA, ACC, LM, PK, RX, RZ, SM, AL,
            hs, hr, fs, fr, rs, rr, xs, xr, zs, zr, gs, gr):
     nc, nx, ny, count, NV, NR, X, Y, NZ = dims
     S = count // 2
+    CH = E.shape[0] // S
+    NC = S * CH
+    W = NV // CH
     R = 2 * Y
     J = X * Y
     K = ny // 2
@@ -35,6 +38,15 @@
     xup = lax.rem(mx + 1, nx)
     xdown = lax.rem(mx + nx - 1, nx)
 
+    def load(src, dst, i):
+        copy = pltpu.make_async_copy(src, dst, ls.at[i])
+        copy.start()
+        return copy
+
+    away = [load(start_h.at[q * S + c], start.at[c], c) for c in range(S)]
+    level_load = load(dis_h, dis, 2 * S)
+    kept = [load(start_h.at[p * S + c], start.at[S + c], S + c) for c in range(S)]
+    ritz_load = load(ritz_h, ritz, 2 * S + 1)
     barrier = pltpu.get_barrier_semaphore()
 
     def greet(dev):
@@ -58,21 +70,18 @@
     greet(cdown)
 
     lo = H + Y * p
+    for c in range(NC):
+        if c % CH == 0:
+            away[c // CH].wait()
+        for x in range(X):
+            for r in range(Y):
+                T[c, x, r] = start[c // CH, pl.ds((c % CH) * W * J + x * Y + r, W, stride=J), :]
+    level_load.wait()
     for x in range(X):
         for r in range(Y):
             row = dis[pl.ds(x * Y + r, 1), :].astype(jnp.float32)
             row = 16.5 * (row / jnp.float32(LEVELS - 1) - 0.5)
             O[H + x, lo + r] = jnp.broadcast_to(row, (8, NZ))
-    for c in range(S):
-        for x in range(X):
-            for r in range(Y):
-                pick = pl.ds(x * Y + r, NV, stride=J)
-                T[c, x, r] = start[q * S + c, pick, :]
-                E[c, H + x, lo + r] = start[p * S + c, pick, :]
-    for s in range(count):
-        for x in range(X):
-            for r in range(Y):
-                RA[s + 1, x, r] = ritz[s, pl.ds(x * Y + r, NR, stride=J), :]
     pl.semaphore_wait(barrier, ng + K)
 
     pending = []
@@ -88,7 +97,7 @@
             src_ref=dst, dst_ref=dst, send_sem=rs_, recv_sem=rs_,
             device_id=(cut, mx, partner), device_id_type=MESH).wait_recv()
 
-    fields = [(S, O)] + [(c, E.at[c]) for c in range(S)]
+    fields = [(NC, O)] + [(c, E.at[c]) for c in range(NC)]
     xi = pl.ds(H, X)
     xy = (cut, mx, partner)
 
@@ -104,19 +113,33 @@
              hs.at[c, 1 + side], hr.at[c, 1 + side], (cut, mx, target))
 
     for c, buf in fields:
-        src = buf.at[xi, row_block(lo)] if c == S else T.at[c]
+        src = buf.at[xi, row_block(lo)] if c == NC else T.at[c]
         send(src, buf.at[xi, row_block(lo)], hs.at[c, 0], hr.at[c, 0], xy)
-    for c, buf in fields:
+    for c in range(NC):
+        if c % CH == 0:
+            kept[c // CH].wait()
+        for x in range(X):
+            for r in range(Y):
+                E[c, H + x, lo + r] = start[S + c // CH, pl.ds((c % CH) * W * J + x * Y + r, W, stride=J), :]
+    for c, buf in fields[:2]:
         send_rows(c, buf, p)
-    send(RA.at[count], RA.at[0], rs.at[0], rr.at[0], cup)
-    send(RA.at[1], RA.at[count + 1], rs.at[1], rr.at[1], cdown)
+    ritz_load.wait()
+    for s in range(count):
+        for x in range(X):
+            for r in range(Y):
+                RA[s + 1, x, r] = ritz[s, pl.ds(x * Y + r, NR, stride=J), :]
 
     own = pl.ds(H, R)
     for c, buf in fields:
         arrived(buf.at[xi, row_block(H + Y * q)], hr.at[c, 0])
         send_rows(c, buf, q)
+        if c < NC - 1:
+            send_rows(c + 1, fields[c + 2][1], p)
         send(buf.at[pl.ds(X, H), own], buf.at[pl.ds(0, H), own], hs.at[c, 3], hr.at[c, 3], (cut, xup, my))
         send(buf.at[pl.ds(H, H), own], buf.at[pl.ds(H + X, H), own], hs.at[c, 4], hr.at[c, 4], (cut, xdown, my))
+
+    send(RA.at[count], RA.at[0], rs.at[0], rr.at[0], cup)
+    send(RA.at[1], RA.at[count + 1], rs.at[1], rr.at[1], cdown)
 
     def point(src, c, x, r, centre):
         v = src(x, r)
@@ -124,7 +147,7 @@
         beside = beside + src(x, r + 1) + src(x, r - 1)
         beside = beside + pltpu.roll(v, 1, 1) + pltpu.roll(v, NZ - 1, 1)
         level = O[x, r] - centre
-        level = jnp.concatenate([level] * (NV // 8), 0)
+        level = jnp.concatenate([level] * (W // 8), 0)
         return (level * v - beside) * 0.0625
 
     for c, buf in fields:
@@ -138,10 +161,11 @@
         for side, row in ((0, 1), (1, H + R)):
             arrived(buf.at[1, row], hr.at[c, 5 + 2 * side])
             arrived(buf.at[H + X, row], hr.at[c, 6 + 2 * side])
-        if c == S:
+        if c == NC:
             continue
-        s = p * S + c
-        centre = (bnd[s, 0] + bnd[s, 1]) / 2.0
+        s = p * S + c // CH
+        part = pl.ds((c % CH) * W, W)
+        centre = (bnd[0, s] + bnd[1, s]) / 2.0
 
         def from_e(x, r, c=c):
             return E[c, x, r]
@@ -160,16 +184,16 @@
 
         lax.fori_loop(0, X, first, 0)
 
-        def second(i, carry, c=c, s=s, centre=centre):
+        def second(i, carry, c=c, s=s, centre=centre, part=part):
             for r in range(Y):
                 a = H + Y * p + r
-                FA[s, i, r] = 2.0 * point(from_u, c, H + i, a, centre) - E[c, H + i, a]
+                FA[s, i, r, part] = 2.0 * point(from_u, c, H + i, a, centre) - E[c, H + i, a]
                 b = H + Y * q + r
                 FT[c, i, r] = 2.0 * point(from_u, c, H + i, b, centre) - E[c, H + i, b]
             return carry
 
         lax.fori_loop(0, X, second, 0)
-        send(FT.at[c], FA.at[s], fs.at[c], fr.at[c], xy)
+        send(FT.at[c], FA.at[s, :, :, part], fs.at[c], fr.at[c], xy)
 
     arrived(RA.at[0], rr.at[0])
     arrived(RA.at[count + 1], rr.at[1])
@@ -182,8 +206,8 @@
     def _():
         RA[count + 1] = jnp.zeros((X, Y, NR, NZ), jnp.float32)
 
-    for c in range(S):
-        arrived(FA.at[q * S + c], fr.at[c])
+    for c in range(NC):
+        arrived(FA.at[q * S + c // CH, :, :, pl.ds((c % CH) * W, W)], fr.at[c])
 
     contract = (((1,), (1,)), ((), ()))
     ACC[...] = jnp.zeros(ACC.shape, jnp.float32)
@@ -328,6 +352,8 @@
     NR = ritz.shape[1]
     J = X * Y
     S, R, K, ng = count // 2, 2 * Y, ny // 2, nx * 2
+    CH = 1
+    NC, W = S * CH, NV // CH
     NL = count * NV + (count + 2) * NR
     tg = -(-((NV + 2 * NR) // 8 * (NL // 128)) // ng)
     f32 = jnp.float32
@@ -335,19 +361,24 @@
     D = pltpu.SemaphoreType.DMA
     dims = (nc, nx, ny, count, NV, NR, X, Y, NZ)
     vm = pl.BlockSpec(memory_space=pltpu.VMEM)
+    hbm = pl.BlockSpec(memory_space=pl.ANY)
     block, corr = pl.pallas_call(
         functools.partial(kernel, dims),
         out_shape=(jax.ShapeDtypeStruct((count, NV * J, NZ), f32),
                    jax.ShapeDtypeStruct((count, 2 * NR, NV), f32)),
-        in_specs=[vm, pl.BlockSpec(memory_space=pltpu.SMEM), vm, vm],
+        in_specs=[hbm, pl.BlockSpec(memory_space=pltpu.SMEM), hbm, hbm],
         out_specs=(vm, vm),
         scratch_shapes=[
-            V((S, X + 2 * H, R + 2 * H, NV, NZ), f32),
-            V((S, X, Y, NV, NZ), f32),
+            V((J, NZ), jnp.int32),
+            V((count, NV * J, NZ), f32),
+            V((count, NR * J, NZ), f32),
+            D((2 * S + 2,)),
+            V((NC, X + 2 * H, R + 2 * H, W, NZ), f32),
+            V((NC, X, Y, W, NZ), f32),
             V((X + 2 * H, R + 2 * H, 8, NZ), f32),
-            V((X + 2 * H, R + 2 * H, NV, NZ), f32),
+            V((X + 2 * H, R + 2 * H, W, NZ), f32),
             V((count, X, Y, NV, NZ), f32),
-            V((S, X, Y, NV, NZ), f32),
+            V((NC, X, Y, W, NZ), f32),
             V((count + 2, X, Y, NR, NZ), f32),
             V((NL, NL), f32),
             V((count, NV, NV + 2 * NR), f32),
@@ -356,11 +387,11 @@
             V((K, tg, 8, 128), f32),
             V((tg, 8, 128), f32),
             V((ng, tg, 8, 128), f32),
-            D((S + 1, 9)), D((S + 1, 9)), D((S,)), D((S,)), D((2,)), D((2,)),
+            D((NC + 1, 9)), D((NC + 1, 9)), D((NC,)), D((NC,)), D((2,)), D((2,)),
             D((ng,)), D((ng,)), D((K,)), D((K,)), D((ng,)), D((ng,)),
         ],
-        compiler_params=pltpu.CompilerParams(collective_id=0, has_side_effects=True, vmem_limit_bytes=48 << 20),
-    )(disorder.reshape(J, NZ), slice_bounds, start.reshape(count, NV * J, NZ), ritz.reshape(count, NR * J, NZ))
+        compiler_params=pltpu.CompilerParams(collective_id=0, has_side_effects=True, vmem_limit_bytes=67043328),
+    )(disorder.reshape(J, NZ), slice_bounds.T, start.reshape(count, NV * J, NZ), ritz.reshape(count, NR * J, NZ))
     return (block.reshape(start.shape), corr)
 
 

time: 84.3 us -> 83.1 us (0.986)
  local copies, waits for them, and re-layouts: 5.63 us -> 3.77 us
    unnamed x9 -> x4, local copies, waits for them, and re-layouts: 5.63 us -> 3.77 us
where the time goes in v2:
time: 83.1 us; the launch traced here: 82.9 us
  Pallas kernels  78.5 us (94%)
  local copies, waits for them, and re-layouts  3.77 us (5%)
    pallas_call x1, Pallas kernels, on_device(): pl.pallas_call(functools.partial(kernel, dims), out_shape=(jax.ShapeDtype...  78.5 us
    unnamed x4, local copies, waits for them, and re-layouts  3.77 us

profile of v2, /device:TPU:0, one launch (start us, length us, event | category | flops | bytes accessed | tf_op | source)
XLA Modules:
  0.0 82.9 jit_solution(12662635849433333346)
XLA Ops:
  0.6 78.5 %shard_map.59 = (f32[6,512,128]{2,1,0:T(8,128)}, f32[6,16,32]{2,1,0:T(8,128)}) custom-call(s32[16,128]{1,0:T(8,128)} %bitcast.8, f32[2,6]{1,0:T(2,128)} %bitcast.9, f32[6,512,128]{2,1,0:T(8,128)} %bitcast.5, f32[6,128,128]{2,1,0:T(8,128)} %bitcast.7), custom_call_target="tpu_custom_call" | custom-call | tf_op jit(solution)/shard_map/pallas_call | solution.py:365
  79.2 0.0 copy-start
  79.2 3.1 %copy.8 = f32[6,32,8,2,128]{4,3,2,1,0:T(2,128)} copy(f32[6,32,8,2,128]{4,3,2,1,0:T(2,128)} %bitcast.6) | data formatting | bytes 3145728
  82.3 0.0 copy-done
  82.3 0.6 copy.9
Async XLA Ops:
  79.2 3.2 %copy-start = (f32[6,16,32]{2,1,0:T(8,128)S(1)}, f32[6,16,32]{2,1,0:T(8,128)}, u32[]{:S(2)}) copy-start(f32[6,16,32]{2,1,0:T(8,128)} %get-tuple-element.9) | copy-start | bytes 36868
